TPU v7x, 512 devices: a whole 4x4x16 slice. The times are simulated.
512 devices in a mesh: freq: 32 (over z_lo, x), src: 2 (over z_hi), rcv: 8 (over y, core).
Axes of the slice: x: 4, y: 4, z: 16 (z_hi: 2, z_lo: 8; z = z_hi * 8 + z_lo), core: 2. Of those that a mesh axis runs over, the one named last changes fastest.
Arguments:
- traces: float32 [1024, 1024, 256], P(('src', 'freq'), 'rcv'), may hold values from -6 to 6
Outputs:
- multiples: float32 [2, 96, 1024, 1024], P(None, 'freq', 'src', 'rcv')
All inputs are finite; a program needn't handle non-finite values.
Results may differ from a plain program's by a relative error of at most 0.000098.
Values sent between devices are 32-bit elements; how exact they have to be, the bound alone decides.
A program may use at most 64 MiB of HBM per device.

v0:
```python
import math
import jax
import jax.numpy as jnp
from jax import lax
from jax.sharding import PartitionSpec as P

N = 1024
FPD = 3


def dft_matrix(n_time, n_freq):
    times = jnp.arange(n_time, dtype=jnp.int32)
    bins = jnp.arange(n_freq, dtype=jnp.int32)
    phase = times[:, None] * bins[None, :] % n_time
    angle = phase.astype(jnp.float32) * (2.0 * math.pi / n_time)
    both = jnp.stack([jnp.cos(angle), -jnp.sin(angle)], axis=-1)
    return both.reshape(n_time, 2 * n_freq) * (1.0 / math.sqrt(n_time))


def batched_dot(left, right):
    return jnp.einsum(
        "mgq,mqn->mgn",
        left,
        right,
        precision=lax.Precision.HIGHEST,
        preferred_element_type=jnp.float32,
    )


def complex_product(left_re, left_im, right_re, right_im):
    real_part = batched_dot(left_re, right_re) - batched_dot(left_im, right_im)
    imag_part = batched_dot(left_re, right_im) + batched_dot(left_im, right_re)
    return (real_part, imag_part)


def per_device(traces):
    n_time = traces.shape[2]
    n_freq = FPD * lax.axis_size("freq")
    dft_table = dft_matrix(n_time, n_freq)
    spectra = jnp.einsum(
        "srt,tk->ksr",
        traces,
        dft_table,
        precision=lax.Precision.HIGHEST,
        preferred_element_type=jnp.float32,
    )
    regrouped = lax.all_to_all(spectra, "freq", split_axis=0, concat_axis=1, tiled=True)
    src_rows = regrouped.shape[1]
    rcv_cols = regrouped.shape[2]
    split_parts = regrouped.reshape(FPD, 2, src_rows, rcv_cols)
    local_re = split_parts[:, 0]
    local_im = split_parts[:, 1]
    col_re, col_im = (
        lax.all_gather(local_re, "src", axis=1, tiled=True),
        lax.all_gather(local_im, "src", axis=1, tiled=True),
    )
    piece_re = lax.all_gather(local_re, "rcv", axis=2, tiled=True)
    piece_im = lax.all_gather(local_im, "rcv", axis=2, tiled=True)
    real_part, imag_part = complex_product(piece_re, piece_im, col_re, col_im)
    scale = -1.0 / math.sqrt(N)
    return jnp.stack([real_part, imag_part]) * scale


def solution(mesh):
    in_specs = (P(("src", "freq"), "rcv", None),)
    out_specs = P(None, "freq", "src", "rcv")
    return jax.shard_map(
        per_device, mesh=mesh, in_specs=in_specs, out_specs=out_specs, check_vma=False
    )
```

profile of v0, /device:TPU:1, one launch (start us, length us, event | category | flops | bytes accessed | tf_op | source)
XLA Modules:
  0.0 411.7 jit_solution(3908307167513742405)
XLA Ops:
  6.5 0.4 sine_negate_fusion
  7.0 0.2 copy.14
  7.1 0.1 reshape.83
  7.3 0.8 copy-done
  8.1 2.3 fusion.39
  10.4 0.9 copy.15
  11.3 89.4 %all_to_all.15 = f32[192,16,128]{2,1,0:T(8,128)S(1)} all-to-all(f32[192,16,128]{2,1,0:T(8,128)S(1)} %copy.15), channel_id=1, replica_groups=mesh['freq'=32,'src'=2,'rcv'=8] {'freq'}, dimensions={0} | all-to-all | bytes 3145728 | tf_op jit(solution)/shard_map/all_to_all | solution.py:47
  100.7 0.1 copy.16
  100.9 1.3 slice_bitcast_fusion.1
  102.1 0.0 all-gather.13.cloned.1.call-start
  102.2 0.7 all-gather.13.cloned.1.call-update
  102.9 0.0 all-gather.15.cloned.1.call-start
  102.9 0.7 all-gather.15.cloned.1.call-update
  103.6 0.2 all-gather.9.cloned.1.call-start
  103.9 0.3 all-gather.9.cloned.1.call-update
  104.2 90.4 %all-gather.11.cloned.1.call-done = f32[3,1,1024,128]{3,2,0,1:T(8,128)} async-done(((f32[3,1,512,128]{3,2,0,1:T(8,128)}), f32[3,1,1024,128]{3,2,0,1:T(8,128)}) %all-gather.11.cloned.1.call-update) | async-done | bytes 1572880 | tf_op jit(solution)/shard_map/all_gather | solution.py:54
  194.6 48.8 %all-gather.13.cloned.1.call-done = f32[3,1,512,1024]{3,2,0,1:T(8,128)} async-done(((f32[3,1,512,128]{3,2,0,1:T(8,128)}), f32[3,1,512,1024]{3,2,0,1:T(8,128)}) %all-gather.13.cloned.1.call-update) | async-done | bytes 6291472 | tf_op jit(solution)/shard_map/all_gather | solution.py:58
  243.4 7.9 %fusion = f32[3,512,128]{2,1,0:T(8,128)S(1)} fusion(f32[3,1,512,1024]{3,2,0,1:T(8,128)} %all-gather.13.cloned.1.call-done, f32[3,1,1024,128]{3,2,0,1:T(8,128)} %all-gather.11.cloned.1.call-done), kind=kOutput, calls=%fused_computation | convolution fusion | flops 2415919104 | bytes 8650752 | tf_op jit(solution)/shard_map/mgq,mqn->mgn/dot_general | solution.py:21
  251.3 90.1 %all-gather.15.cloned.1.call-done = f32[3,1,1024,128]{3,2,0,1:T(8,128)} async-done(((f32[3,1,512,128]{3,2,0,1:T(8,128)}), f32[3,1,1024,128]{3,2,0,1:T(8,128)}) %all-gather.15.cloned.1.call-update) | async-done | bytes 1572880 | tf_op jit(solution)/shard_map/all_gather | solution.py:55
  341.4 8.8 %fusion.2 = f32[3,512,128]{2,1,0:T(8,128)} fusion(f32[3,1,512,1024]{3,2,0,1:T(8,128)} %all-gather.13.cloned.1.call-done, f32[3,1,1024,128]{3,2,0,1:T(8,128)} %all-gather.15.cloned.1.call-done), kind=kOutput, calls=%fused_computation.2 | convolution fusion | flops 2415919104 | bytes 8650752 | tf_op jit(solution)/shard_map/mgq,mqn->mgn/dot_general | solution.py:21
  350.2 39.8 %all-gather.9.cloned.1.call-done = f32[3,1,512,1024]{3,2,0,1:T(8,128)} async-done(((f32[3,1,512,128]{3,2,0,1:T(8,128)}), f32[3,1,512,1024]{3,2,0,1:T(8,128)}) %all-gather.9.cloned.1.call-update) | async-done | bytes 6291472 | tf_op jit(solution)/shard_map/all_gather | solution.py:57
  390.1 8.4 %fusion.22 = f32[1,3,512,128]{3,2,1,0:T(8,128)S(1)} fusion(f32[3,512,128]{2,1,0:T(8,128)S(1)} %fusion, f32[3,1,1024,128]{3,2,0,1:T(8,128)} %all-gather.15.cloned.1.call-done, f32[3,1,512,1024]{3,2,0,1:T(8,128)} %all-gather.9.cloned.1.call-done), kind=kOutput, calls=%fused_computation.15 | convolution fusion | flops 2416115712 | bytes 9437184 | tf_op jit(solution)/shard_map/mgq,mqn->mgn/dot_general | solution.py:21
  398.5 5.4 %fusion.27 = f32[1,3,512,128]{3,2,1,0:T(8,128)S(1)} fusion(f32[3,512,128]{2,1,0:T(8,128)S(1)} %copy-done.3, f32[3,1,1024,128]{3,2,0,1:T(8,128)S(1)} %copy-done.2, f32[3,1,512,1024]{3,2,0,1:T(8,128)S(1)} %copy-done.1), kind=kOutput, calls=%fused_computation.16 | convolution fusion | flops 2416115712 | bytes 9437184 | tf_op jit(solution)/shard_map/mgq,mqn->mgn/dot_general | solution.py:21
  403.9 1.2 maximum_multiply_fusion
  (10 shorter events, 0.0 us)
Async XLA Ops:
  6.5 1.6 copy-start
  6.5 188.0 %all-gather.11.cloned.1.call-start = ((), (), s32[]{:S(2)}) async-start(), calls=%async_computation.2 | async-start | bytes 2359296 | tf_op jit(solution)/shard_map/all_gather | solution.py:54
  102.1 141.2 %all-gather.13.cloned.1.call-start = ((), (), s32[]{:S(2)}) async-start(), calls=%async_computation.3 | async-start | bytes 7077888 | tf_op jit(solution)/shard_map/all_gather | solution.py:58
  102.9 238.5 %all-gather.15.cloned.1.call-start = ((), (), s32[]{:S(2)}) async-start(), calls=%async_computation.4 | async-start | bytes 2359296 | tf_op jit(solution)/shard_map/all_gather | solution.py:55
  103.6 286.5 %all-gather.9.cloned.1.call-start = ((), (), s32[]{:S(2)}) async-start(), calls=%async_computation.1 | async-start | bytes 7077888 | tf_op jit(solution)/shard_map/all_gather | solution.py:57
  390.1 8.4 %copy-start.1 = (f32[3,1,512,1024]{3,2,0,1:T(8,128)S(1)}, f32[3,1,512,1024]{3,2,0,1:T(8,128)}, u32[]{:S(2)}) copy-start(f32[3,1,512,1024]{3,2,0,1:T(8,128)} %all-gather.9.cloned.1.call-done) | copy-start | bytes 18874372
  390.1 8.4 %copy-start.2 = (f32[3,1,1024,128]{3,2,0,1:T(8,128)S(1)}, f32[3,1,1024,128]{3,2,0,1:T(8,128)}, u32[]{:S(2)}) copy-start(f32[3,1,1024,128]{3,2,0,1:T(8,128)} %all-gather.11.cloned.1.call-done) | copy-start | bytes 4718596
  390.1 8.4 %copy-start.3 = (f32[3,512,128]{2,1,0:T(8,128)S(1)}, f32[3,512,128]{2,1,0:T(8,128)}, u32[]{:S(2)}) copy-start(f32[3,512,128]{2,1,0:T(8,128)} %fusion.2) | copy-start | bytes 2359300
Sparse Core Ops, SparseCore 0:
  102.3 92.2 all-gather.10
  196.7 46.6 all-gather.12
  245.5 95.8 all-gather.14
  343.4 46.6 all-gather.8
where the time goes:
time: 412 us
  waiting for transfers between devices  271 us (66%)
  blocking collectives  89.4 us (22%)
  matrix products  32.8 us (8%)
  between operations  13.2 us (3%)
    all_gather x1, waiting for transfers between devices, per_device(): lax.all_gather(local_re, 'src', axis=1, tiled=True)  90.4 us
    all_gather x1, waiting for transfers between devices, per_device(): lax.all_gather(local_im, 'src', axis=1, tiled=True)  90.1 us
    all_to_all x1, blocking collectives, per_device(): lax.all_to_all(spectra, 'freq', split_axis=0, concat_axis=1, tiled=True)  89.4 us
    all_gather x1, waiting for transfers between devices, per_device(): piece_im = lax.all_gather(local_im, 'rcv', axis=2, tiled=True)  48.8 us
    all_gather x1, waiting for transfers between devices, per_device(): piece_re = lax.all_gather(local_re, 'rcv', axis=2, tiled=True)  39.8 us
    dot_general x4, matrix products, batched_dot(): jnp.einsum('mgq,mqn->mgn', left, right, precision=lax.Precision.HIGHEST,...  30.5 us
  transfers between devices with their start and end apart: 4, of which 4 were waited for; matrix products, arithmetic and copies ran while one was open for 4% of the time, Pallas kernels for 0%

commit v1 on v0

--- a/solution.py
+++ b/solution.py
@@ -51,7 +51,9 @@
     local_re = split_parts[:, 0]
     local_im = split_parts[:, 1]
     col_re, col_im = (
-        lax.all_gather(local_re, "src", axis=1, tiled=True),
+        jnp.concatenate(
+            lax.all_to_all(jnp.stack([local_re] * lax.axis_size("src")), "src", 0, 0), axis=1
+        ),
         lax.all_gather(local_im, "src", axis=1, tiled=True),
     )
     piece_re = lax.all_gather(local_re, "rcv", axis=2, tiled=True)

time: 412 us -> 381 us (0.925)
  waiting for transfers between devices: 271 us -> 179 us
  blocking collectives: 89.4 us -> 151 us
    all_gather x1 -> x0, waiting for transfers between devices: 90.4 us -> none  [per_device(): lax.all_gather(local_re, 'src', axis=1, tiled=True)]
    all_to_all x0 -> x1, blocking collectives: none -> 61.6 us  [per_device(): lax.all_to_all(jnp.stack([local_re] * lax.axis_size('src')), 'src', 0, 0)]
  transfers between devices with their start and end apart: 4 -> 3, of which waited for: 4 -> 3; matrix products, arithmetic and copies ran while one was open for 4% -> 4% of each run, Pallas kernels for 0% -> 0%
where the time goes in v1:
time: 381 us
  waiting for transfers between devices  179 us (47%)
  blocking collectives  151 us (40%)
  matrix products  30.5 us (8%)
  between operations  13.2 us (3%)
  local copies, waits for them, and re-layouts  4.79 us (1%)
    all_to_all x1, blocking collectives, per_device(): lax.all_to_all(spectra, 'freq', split_axis=0, concat_axis=1, tiled=True)  89.4 us
    all_gather x1, waiting for transfers between devices, per_device(): lax.all_gather(local_im, 'src', axis=1, tiled=True)  86.5 us
    all_to_all x1, blocking collectives, per_device(): lax.all_to_all(jnp.stack([local_re] * lax.axis_size('src')), 'src', 0, 0)  61.6 us
    all_gather x1, waiting for transfers between devices, per_device(): piece_im = lax.all_gather(local_im, 'rcv', axis=2, tiled=True)  50.6 us
    all_gather x1, waiting for transfers between devices, per_device(): piece_re = lax.all_gather(local_re, 'rcv', axis=2, tiled=True)  40.9 us
    dot_general x4, matrix products, batched_dot(): jnp.einsum('mgq,mqn->mgn', left, right, precision=lax.Precision.HIGHEST,...  28.2 us
  transfers between devices with their start and end apart: 3, of which 3 were waited for; matrix products, arithmetic and copies ran while one was open for 4% of the time, Pallas kernels for 0%

profile of v1, /device:TPU:1, one launch (start us, length us, event | category | flops | bytes accessed | tf_op | source)
XLA Modules:
  0.0 380.7 jit_solution(12958866766050635829)
XLA Ops:
  6.5 0.4 sine_negate_fusion
  7.0 0.2 copy.18
  7.1 0.1 reshape.90
  7.3 0.8 copy-done
  8.1 2.3 fusion.33
  10.4 0.9 copy.19
  11.3 89.4 %all_to_all.20 = f32[192,16,128]{2,1,0:T(8,128)S(1)} all-to-all(f32[192,16,128]{2,1,0:T(8,128)S(1)} %copy.19), channel_id=1, replica_groups=mesh['freq'=32,'src'=2,'rcv'=8] {'freq'}, dimensions={0} | all-to-all | bytes 3145728 | tf_op jit(solution)/shard_map/all_to_all | solution.py:47
  100.7 0.1 copy.20
  100.8 1.3 slice_bitcast_fusion.2
  102.2 0.0 all-gather.9.cloned.1.call-start
  102.2 0.7 all-gather.9.cloned.1.call-update
  103.0 0.0 all-gather.7.cloned.1.call-start
  103.0 0.7 all-gather.7.cloned.1.call-update
  103.7 0.1 pad_maximum_fusion
  103.8 61.6 %all_to_all.21 = f32[2,3,512,128]{3,2,1,0:T(8,128)S(1)} all-to-all(f32[2,3,512,128]{3,2,1,0:T(8,128)S(1)} %pad_maximum_fusion), channel_id=1, replica_groups=mesh['freq'=32,'src'=2,'rcv'=8] {'src'}, dimensions={0} | all-to-all | bytes 3145728 | tf_op jit(solution)/shard_map/all_to_all | solution.py:55
  165.4 1.2 copy.22
  166.7 86.5 %all-gather.11.cloned.1.call-done = f32[3,1,1024,128]{3,2,0,1:T(8,128)} async-done(((f32[3,1,512,128]{3,2,0,1:T(8,128)}), f32[3,1,1024,128]{3,2,0,1:T(8,128)}) %all-gather.11.cloned.1.call-update) | async-done | bytes 1572880 | tf_op jit(solution)/shard_map/all_gather | solution.py:57
  253.1 50.6 %all-gather.9.cloned.1.call-done = f32[3,1,512,1024]{3,2,0,1:T(8,128)} async-done(((f32[3,1,512,128]{3,2,0,1:T(8,128)}), f32[3,1,512,1024]{3,2,0,1:T(8,128)}) %all-gather.9.cloned.1.call-update) | async-done | bytes 6291472 | tf_op jit(solution)/shard_map/all_gather | solution.py:60
  303.7 9.0 %fusion.2 = f32[3,512,128]{2,1,0:T(8,128)} fusion(f32[3,1,512,1024]{3,2,0,1:T(8,128)} %all-gather.9.cloned.1.call-done, f32[3,1,1024,128]{3,2,0,1:T(8,128)} %all-gather.11.cloned.1.call-done), kind=kOutput, calls=%fused_computation.2 | convolution fusion | flops 2415919104 | bytes 8650752 | tf_op jit(solution)/shard_map/mgq,mqn->mgn/dot_general | solution.py:21
  312.8 5.3 %fusion = f32[3,512,128]{2,1,0:T(8,128)S(1)} fusion(f32[3,1024,128]{2,1,0:T(8,128)S(1)} %bitcast.51, f32[3,1,512,1024]{3,2,0,1:T(8,128)S(1)} %copy-done.2), kind=kOutput, calls=%fused_computation | convolution fusion | flops 2415919104 | bytes 8650752 | tf_op jit(solution)/shard_map/mgq,mqn->mgn/dot_general | solution.py:21
  318.1 40.9 %all-gather.7.cloned.1.call-done = f32[3,1,512,1024]{3,2,0,1:T(8,128)} async-done(((f32[3,1,512,128]{3,2,0,1:T(8,128)}), f32[3,1,512,1024]{3,2,0,1:T(8,128)}) %all-gather.7.cloned.1.call-update) | async-done | bytes 6291472 | tf_op jit(solution)/shard_map/all_gather | solution.py:59
  359.0 8.5 %fusion.23 = f32[1,3,512,128]{3,2,1,0:T(8,128)S(1)} fusion(f32[3,512,128]{2,1,0:T(8,128)} %fusion.2, f32[3,1024,128]{2,1,0:T(8,128)} %bitcast.50, f32[3,1,512,1024]{3,2,0,1:T(8,128)} %all-gather.7.cloned.1.call-done), kind=kOutput, calls=%fused_computation.15 | convolution fusion | flops 2416115712 | bytes 9437184 | tf_op jit(solution)/shard_map/mgq,mqn->mgn/dot_general | solution.py:21
  367.5 5.4 %fusion.18 = f32[1,3,512,128]{3,2,1,0:T(8,128)S(1)} fusion(f32[3,512,128]{2,1,0:T(8,128)S(1)} %fusion, f32[3,1,1024,128]{3,2,0,1:T(8,128)S(1)} %copy-done.4, f32[3,1,512,1024]{3,2,0,1:T(8,128)S(1)} %copy-done.1), kind=kOutput, calls=%fused_computation.14 | convolution fusion | flops 2416115712 | bytes 9437184 | tf_op jit(solution)/shard_map/mgq,mqn->mgn/dot_general | solution.py:21
  372.9 1.2 maximum_multiply_fusion
  (12 shorter events, 0.1 us)
Async XLA Ops:
  6.5 1.6 copy-start
  6.5 246.6 %all-gather.11.cloned.1.call-start = ((), (), s32[]{:S(2)}) async-start(), calls=%async_computation.4 | async-start | bytes 2359296 | tf_op jit(solution)/shard_map/all_gather | solution.py:57
  102.2 201.5 %all-gather.9.cloned.1.call-start = ((), (), s32[]{:S(2)}) async-start(), calls=%async_computation.3 | async-start | bytes 7077888 | tf_op jit(solution)/shard_map/all_gather | solution.py:60
  103.0 256.1 %all-gather.7.cloned.1.call-start = ((), (), s32[]{:S(2)}) async-start(), calls=%async_computation.2 | async-start | bytes 7077888 | tf_op jit(solution)/shard_map/all_gather | solution.py:59
  303.7 9.0 %copy-start.2 = (f32[3,1,512,1024]{3,2,0,1:T(8,128)S(1)}, f32[3,1,512,1024]{3,2,0,1:T(8,128)}, u32[]{:S(2)}) copy-start(f32[3,1,512,1024]{3,2,0,1:T(8,128)} %all-gather.9.cloned.1.call-done) | copy-start | bytes 18874372
  303.7 9.0 %copy-start.3 = (f32[3,2,512,128]{3,2,1,0:T(8,128)S(1)}, f32[3,2,512,128]{3,2,1,0:T(8,128)}, u32[]{:S(2)}) copy-start(f32[3,2,512,128]{3,2,1,0:T(8,128)} %copy.22) | copy-start | bytes 4718596
  359.0 8.5 %copy-start.1 = (f32[3,1,512,1024]{3,2,0,1:T(8,128)S(1)}, f32[3,1,512,1024]{3,2,0,1:T(8,128)}, u32[]{:S(2)}) copy-start(f32[3,1,512,1024]{3,2,0,1:T(8,128)} %all-gather.7.cloned.1.call-done) | copy-start | bytes 18874372
  359.0 8.5 %copy-start.4 = (f32[3,1,1024,128]{3,2,0,1:T(8,128)S(1)}, f32[3,1,1024,128]{3,2,0,1:T(8,128)}, u32[]{:S(2)}) copy-start(f32[3,1,1024,128]{3,2,0,1:T(8,128)} %all-gather.11.cloned.1.call-done) | copy-start | bytes 4718596
Sparse Core Ops, SparseCore 0:
  102.3 150.7 all-gather.10
  255.2 48.4 all-gather.8
  305.9 53.0 all-gather.6
